TPU v7x, 32 devices: a whole 2x2x4 slice. The times are simulated.
32 devices in a mesh: grp: 4 (over y, x), pos: 8 (over z, core).
Axes of the slice: x: 2, y: 2, z: 4, core: 2. Of those that a mesh axis runs over, the one named last changes fastest.
Arguments:
- tiles: float32 [4, 8, 12, 256, 256], P('grp', 'pos'), may hold values from -0.109375 to 0.109375
- tile_row: int32 [4, 8, 12], P('grp', 'pos'), may hold values from 0 to 7
- tile_col: int32 [4, 8, 12], P('grp', 'pos'), may hold values from 0 to 7
- tile_count: int32 [4, 8], P('grp', 'pos'), may hold values from 1 to 12, as said below
- energies: float32 [16384], P('pos'), may hold values from 1 to 10
- basis: float32 [16, 16384], P(None, 'pos'), may hold values from -6 to 6
- prev_basis: float32 [16, 16384], P(None, 'pos'), may hold values from -6 to 6
- beta_prev: float32 [16, 16], replicated, may hold values from -3 to 3
Outputs:
- next_basis: float32 [16, 16384], P(None, 'pos')
- alpha: float32 [16, 16], replicated
- beta: float32 [16, 16], replicated
Inputs may be any that keep to these rules, and one draw needn't show every extreme that they name: `tile_count`: some segment of some diagonal uses all 12 slots in every draw.
All inputs are finite; a program needn't handle non-finite values.
Results may differ from a plain program's by a relative error of at most 0.00021.
Values sent between devices are 32-bit elements; how exact they have to be, the bound alone decides.
A program may use at most 64 MiB of HBM per device.

v0:
```python
import jax
import jax.numpy as jnp
from jax import lax
from jax.sharding import PartitionSpec as P


def passed_along(array, axis, by):
    peers = lax.axis_size(axis)
    return lax.ppermute(array, axis, [(i, (i + by) % peers) for i in range(peers)])


def matmul(left, right):
    return jnp.dot(left, right, precision=lax.Precision.HIGHEST)


def product(left, right):
    return jnp.dot(left, right.T, precision=lax.Precision.HIGHEST)


def rotate(values_in, offset):
    return passed_along(values_in, "pos", offset)


def shards(tiles, tile_row, tile_col, tile_count, energies, basis, prev_basis, beta_prev):
    slot_count = tiles.shape[2]
    tile_width = tiles.shape[-1]
    blocks = tiles.reshape(slot_count, tile_width, tile_width)
    vector_count, seg_len = basis.shape
    per_side = seg_len // tile_width
    highest = lax.Precision.HIGHEST
    live_mask = (jnp.arange(slot_count, dtype=jnp.int32) < tile_count.reshape(())).astype(
        jnp.float32
    )
    sides = jnp.arange(per_side, dtype=jnp.int32)
    row_hot = (tile_row.reshape(slot_count)[:, None] == sides[None, :]).astype(
        jnp.float32
    ) * live_mask[:, None]
    col_hot = (tile_col.reshape(slot_count)[:, None] == sides[None, :]).astype(
        jnp.float32
    ) * live_mask[:, None]
    own_rows = basis.reshape(vector_count, per_side, tile_width)
    group_index = lax.axis_index("grp")
    bit_count = lax.axis_size("grp").bit_length() - 1
    seg_total = lax.axis_size("pos")
    total_rows = float(seg_len * seg_total)

    def pick(level, arrived, kept):
        return jnp.where(group_index // (1 << level) % 2 == 1, arrived, kept)

    far_rows = own_rows
    for level in range(bit_count):
        far_rows = pick(level, rotate(far_rows, -(1 << level)), far_rows)
    picked = jnp.einsum("kt,btj->kbj", col_hot, far_rows, precision=highest)
    parts = jnp.einsum("kbj,kij->kbi", picked, blocks, precision=highest)
    forward = jnp.einsum("kt,kbi->bti", row_hot, parts, precision=highest)
    picked = jnp.einsum("kt,bti->kbi", row_hot, own_rows, precision=highest)
    parts = jnp.einsum("kbi,kij->kbj", picked, blocks, precision=highest)
    back_rows = jnp.einsum("kt,kbj->btj", col_hot, parts, precision=highest)
    for level in range(bit_count):
        back_rows = pick(level, rotate(back_rows, 1 << level), back_rows)
    partial_sum = (forward + back_rows).reshape(vector_count, seg_len)
    applied = lax.psum(partial_sum, "grp") + energies[None, :] * basis
    alpha = lax.psum(product(basis, applied), "pos") / total_rows
    residual = applied - matmul(alpha.T, basis) - matmul(beta_prev, prev_basis)
    gram = lax.psum(product(residual, residual), "pos") / total_rows
    factor = jnp.linalg.cholesky(gram)
    next_rows = jax.scipy.linalg.solve_triangular(factor, residual, lower=True)
    return (next_rows, alpha, factor)


def solution(mesh):
    in_specs = (
        P("grp", "pos", None, None, None),
        P("grp", "pos", None),
        P("grp", "pos", None),
        P("grp", "pos"),
        P("pos"),
        P(None, "pos"),
        P(None, "pos"),
        P(),
    )
    out_specs = (P(None, "pos"), P(), P())
    return jax.shard_map(shards, mesh=mesh, in_specs=in_specs, out_specs=out_specs, check_vma=False)
```

profile of v0, /device:TPU:0, one launch (start us, length us, event | category | flops | bytes accessed | tf_op | source)
XLA Modules:
  0.0 120.1 jit_solution(79853631742649549)
XLA Ops:
  7.2 0.0 copy-start
  7.2 0.0 all-reduce.2.cloned.1.call-start
  7.2 1.1 copy.19
  8.3 4.6 %collective-permute-start = (f32[16,8,256]{2,1,0:T(8,128)S(1)}, f32[16,8,256]{2,1,0:T(8,128)}, u32[]{:S(2)}, u32[]{:S(2)}) collective-permute-start(f32[16,8,256]{2,1,0:T(8,128)S(1)} %bitcast.48), channel_id=1, source_target_pairs={{0,7},{1,0},{2,1},{3,2},{4,3},{5,4},{6,5},{7,6},{8,15},{9,8},{10,9... | collective-permute-start | bytes 393224 | tf_op jit(solution)/shard_map/ppermute | solution.py:9
  13.6 1.1 fusion.15
  14.7 1.7 %fusion = f32[12,16,256]{2,1,0:T(8,128)S(1)} fusion(f32[1,1,12,256,256]{4,3,2,1,0:T(8,128)S(1)} %copy-done, f32[12,16,256]{2,0,1:T(8,128)S(1)} %fusion.15), kind=kOutput, calls=%fused_computation | convolution fusion | flops 150994944 | bytes 3538944 | tf_op jit(solution)/shard_map/kbi,kij->kbj/dot_general | solution.py:57
  16.4 0.4 convolution_bitcast_fusion
  16.8 0.1 collective-permute-start.2
  17.0 1.1 collective-permute-start.1
  18.0 5.2 %collective-permute-done.2 = f32[16,8,256]{2,1,0:T(8,128)} collective-permute-done((f32[16,8,256]{2,1,0:T(8,128)S(1)}, f32[16,8,256]{2,1,0:T(8,128)}, u32[]{:S(2)}, u32[]{:S(2)}) %collective-permute-start.2) | collective-permute-done | bytes 131104 | tf_op jit(solution)/shard_map/ppermute | solution.py:9
  23.3 0.1 collective-permute-start.3
  23.4 0.0 collective-permute-done.1
  23.4 0.4 fusion.8
  23.8 2.8 %fusion.2 = f32[12,16,256]{2,1,0:T(8,128)S(1)} fusion(f32[1,1,12,256,256]{4,3,2,1,0:T(8,128)S(1)} %copy-done, f32[12,16,256]{2,0,1:T(8,128)S(1)} %fusion.8), kind=kOutput, calls=%fused_computation.2 | convolution fusion | flops 150994944 | bytes 3538944 | tf_op jit(solution)/shard_map/kbj,kij->kbi/dot_general | solution.py:54
  26.6 1.1 convolution_bitcast_fusion.1
  27.7 2.5 %collective-permute-done.3 = f32[16,8,256]{2,1,0:T(8,128)S(1)} collective-permute-done((f32[16,8,256]{2,1,0:T(8,128)S(1)}, f32[16,8,256]{2,1,0:T(8,128)S(1)}, u32[]{:S(2)}, u32[]{:S(2)}) %collective-permute-start.3) | collective-permute-done | bytes 131104 | tf_op jit(solution)/shard_map/ppermute | solution.py:9
  30.2 0.7 copy.20
  30.9 0.0 all-reduce.2.cloned.1.call-update
  30.9 42.9 %all-reduce.2.cloned.1.call-done = f32[16,2048]{1,0:T(8,128)} async-done(((f32[16,2048]{1,0:T(8,128)}), f32[16,2048]{1,0:T(8,128)}) %all-reduce.2.cloned.1.call-update) | async-done | bytes 131088 | tf_op jit(solution)/shard_map/psum | solution.py:62
  73.9 1.2 convolution_bitcast_fusion.2
  75.0 16.2 %psum.22 = f32[16,16]{0,1:T(8,128)S(1)} all-reduce(f32[16,16]{0,1:T(8,128)S(1)} %convolution_bitcast_fusion.2), channel_id=1, replica_groups=mesh['grp'=4,'pos'=8] {'pos'}, use_global_device_ids=true, to_apply=%region_1.2 | all-reduce | flops 256 | bytes 2048 | tf_op jit(solution)/shard_map/psum | solution.py:63
  91.2 0.7 copy.13
  91.9 1.2 convolution_subtract_fusion.1
  93.1 0.3 convolution_subtract_fusion
  93.4 0.2 fusion.40
  93.6 14.0 %psum.23 = f32[16,16]{0,1:T(8,128)S(1)} all-reduce(f32[16,16]{0,1:T(8,128)S(1)} %fusion.40), channel_id=1, replica_groups=mesh['grp'=4,'pos'=8] {'pos'}, use_global_device_ids=true, to_apply=%region_2.3 | all-reduce | flops 256 | bytes 2048 | tf_op jit(solution)/shard_map/psum | solution.py:65
  107.6 0.1 copy.12
  107.7 1.5 %cholesky.16 = f32[16,16]{1,0:T(8,128)S(1)} custom-call(f32[16,16]{1,0:T(8,128)S(1)} %fusion.14), custom_call_target="Cholesky" | custom-call | tf_op jit(solution)/shard_map/jit(cholesky)/cholesky | solution.py:66
  109.1 0.6 compare_reduce_fusion
  109.8 1.2 %select_bitcast_fusion = (f32[1,16,16]{2,1,0:T(8,128)S(1)}, f32[16,16]{1,0:T(8,128)}) fusion(f32[16,16]{1,0:T(8,128)S(1)} %cholesky.16, pred[]{:T(512)} %compare_reduce_fusion), kind=kLoop, calls=%fused_computation.25 | loop fusion | flops 1024 | bytes 3073 | tf_op jit(solution)/shard_map/jit(_solve_triangular)/triangular_solve | solution.py:67
  111.0 1.2 %custom-call.7 = f32[1,16,16]{1,2,0:T(8,128)S(1)} custom-call(f32[1,16,16]{2,1,0:T(8,128)S(1)} %get-tuple-element.6), custom_call_target="InvertDiagBlocksLowerTriangular" | custom-call | tf_op jit(solution)/shard_map/jit(_solve_triangular)/triangular_solve | solution.py:67
  112.3 1.0 fusion.12
  (20 shorter events, 0.2 us)
Async XLA Ops:
  7.2 7.5 %copy-start = (f32[1,1,12,256,256]{4,3,2,1,0:T(8,128)S(1)}, f32[1,1,12,256,256]{4,3,2,1,0:T(8,128)}, u32[]{:S(2)}) copy-start(f32[1,1,12,256,256]{4,3,2,1,0:T(8,128)} %param.8) | copy-start | bytes 9437188
  7.2 9.2 %copy-start.5 = (s32[1,1,12]{2,1,0:T(1,128)S(1)}, s32[1,1,12]{2,1,0:T(1,128)}, u32[]{:S(2)}) copy-start(s32[1,1,12]{2,1,0:T(1,128)} %param.10) | copy-start | bytes 148
  7.2 66.7 %all-reduce.2.cloned.1.call-start = ((), (), s32[]{:S(2)}) async-start(), calls=%async_computation | async-start | bytes 262144 | tf_op jit(solution)/shard_map/psum | solution.py:62
  8.3 8.6 %collective-permute-start = (f32[16,8,256]{2,1,0:T(8,128)S(1)}, f32[16,8,256]{2,1,0:T(8,128)}, u32[]{:S(2)}, u32[]{:S(2)}) collective-permute-start(f32[16,8,256]{2,1,0:T(8,128)S(1)} %bitcast.48), channel_id=1, source_target_pairs={{0,7},{1,0},{2,1},{3,2},{4,3},{5,4},{6,5},{7,6},{8,15},{9,8},{10,9... | collective-permute-start | bytes 393224 | tf_op jit(solution)/shard_map/ppermute | solution.py:9
  16.8 57.0 %copy-start.1 = (f32[16,2048]{1,0:T(8,128)S(1)}, f32[16,2048]{1,0:T(8,128)}, u32[]{:S(2)}) copy-start(f32[16,2048]{1,0:T(8,128)} %param.13) | copy-start | bytes 393220
  16.8 57.0 %copy-start.3 = (f32[2048]{0:T(1024)S(1)}, f32[2048]{0:T(1024)}, u32[]{:S(2)}) copy-start(f32[2048]{0:T(1024)} %param.12) | copy-start | bytes 24580
  16.8 6.5 %collective-permute-start.2 = (f32[16,8,256]{2,1,0:T(8,128)S(1)}, f32[16,8,256]{2,1,0:T(8,128)}, u32[]{:S(2)}, u32[]{:S(2)}) collective-permute-start(f32[16,8,256]{2,1,0:T(8,128)S(1)} %convolution_bitcast_fusion), channel_id=1, source_target_pairs={{0,1},{1,2},{2,3},{3,4},{4,5},{5,6},{6,7},{7,0},{8,9},{9,10},{10,1... | collective-permute-start | bytes 393224 | tf_op jit(solution)/shard_map/ppermute | solution.py:9
  17.0 6.4 %collective-permute-start.1 = (f32[16,8,256]{2,1,0:T(8,128)S(1)}, f32[16,8,256]{2,1,0:T(8,128)S(1)}, u32[]{:S(2)}, u32[]{:S(2)}) collective-permute-start(f32[16,8,256]{2,1,0:T(8,128)S(1)} %broadcast_select_fusion.1), channel_id=1, source_target_pairs={{0,6},{1,7},{2,0},{3,1},{4,2},{5,3},{6,4},{7,5},{8,14},{9,15},{10,... | collective-permute-start | bytes 393224 | tf_op jit(solution)/shard_map/ppermute | solution.py:9
  23.3 69.8 %copy-start.2 = (f32[16,2048]{1,0:T(8,128)S(1)}, f32[16,2048]{1,0:T(8,128)}, u32[]{:S(2)}) copy-start(f32[16,2048]{1,0:T(8,128)} %param.14) | copy-start | bytes 393220
  23.3 69.8 %copy-start.4 = (f32[16,16]{1,0:T(8,128)S(1)}, f32[16,16]{1,0:T(8,128)}, u32[]{:S(2)}) copy-start(f32[16,16]{1,0:T(8,128)} %param.15) | copy-start | bytes 3076
  23.3 6.8 %collective-permute-start.3 = (f32[16,8,256]{2,1,0:T(8,128)S(1)}, f32[16,8,256]{2,1,0:T(8,128)S(1)}, u32[]{:S(2)}, u32[]{:S(2)}) collective-permute-start(f32[16,8,256]{2,1,0:T(8,128)S(1)} %broadcast_select_fusion), channel_id=1, source_target_pairs={{0,2},{1,3},{2,4},{3,5},{4,6},{5,7},{6,0},{7,1},{8,10},{9,11},{10,... | collective-permute-start | bytes 393224 | tf_op jit(solution)/shard_map/ppermute | solution.py:9
Sparse Core Ops, SparseCore 0:
  31.0 42.7 all-reduce.1
where the time goes:
time: 120 us
  waiting for transfers between devices  50.7 us (42%)
  blocking collectives  30.2 us (25%)
  between operations  14.9 us (12%)
  matrix products  11.3 us (9%)
  starting transfers between devices  5.78 us (5%)
  other arithmetic  4.7 us (4%)
  local copies, waits for them, and re-layouts  2.58 us (2%)
    psum x1, waiting for transfers between devices, shards(): applied = lax.psum(partial_sum, 'grp') + energies[None, :] * basis  42.9 us
    psum x1, blocking collectives, shards(): alpha = lax.psum(product(basis, applied), 'pos') / total_rows  16.2 us
    psum x1, blocking collectives, shards(): gram = lax.psum(product(residual, residual), 'pos') / total_rows  14 us
    ppermute x4, waiting for transfers between devices, passed_along(): lax.ppermute(array, axis, [(i, (i + by) % peers) for i in range(peers)])  7.71 us
    ppermute x4, starting transfers between devices, passed_along(): lax.ppermute(array, axis, [(i, (i + by) % peers) for i in range(peers)])  5.74 us
    dot_general x1, matrix products, shards(): parts = jnp.einsum('kbj,kij->kbi', picked, blocks, precision=highest)  2.76 us
    unnamed x15, local copies, waits for them, and re-layouts  2.51 us
    another operation x2, other arithmetic, shards(): next_rows = jax.scipy.linalg.solve_triangular(factor, residual, lower=True)  2.47 us
  transfers between devices with their start and end apart: 5, of which 3 were waited for; matrix products, arithmetic and copies ran while one was open for 6% of the time, Pallas kernels for 0%

commit v1 on v0

--- a/solution.py
+++ b/solution.py
@@ -59,7 +59,7 @@
     for level in range(bit_count):
         back_rows = pick(level, rotate(back_rows, 1 << level), back_rows)
     partial_sum = (forward + back_rows).reshape(vector_count, seg_len)
-    applied = lax.psum(partial_sum, "grp") + energies[None, :] * basis
+    applied = jnp.sum(lax.all_gather(partial_sum, "grp"), axis=0) + energies[None, :] * basis
     alpha = lax.psum(product(basis, applied), "pos") / total_rows
     residual = applied - matmul(alpha.T, basis) - matmul(beta_prev, prev_basis)
     gram = lax.psum(product(residual, residual), "pos") / total_rows

time: 120 us -> 72.9 us (0.61)
  waiting for transfers between devices: 50.7 us -> 7.69 us
  between operations: 14.9 us -> 1.52 us
  blocking collectives: 30.2 us -> 39.6 us
    psum x1 -> x0, waiting for transfers between devices: 42.9 us -> none  [shards(): applied = lax.psum(partial_sum, 'grp') + energies[None, :] * basis]
    all_gather x0 -> x1, blocking collectives: none -> 11.7 us  [shards(): lax.all_gather(partial_sum, 'grp')]
    psum x1, blocking collectives: 16.2 us -> 14 us  [shards(): alpha = lax.psum(product(basis, applied), 'pos') / total_rows]
    unnamed x15 -> x10, local copies, waits for them, and re-layouts: 2.51 us -> 1.8 us
  transfers between devices with their start and end apart: 5 -> 4, of which waited for: 3 -> 2; matrix products, arithmetic and copies ran while one was open for 6% -> 10% of each run, Pallas kernels for 0% -> 0%
where the time goes in v1:
time: 72.9 us; the launch traced here: 72.6 us
  blocking collectives  39.6 us (54%)
  matrix products  10.4 us (14%)
  waiting for transfers between devices  7.69 us (11%)
  other arithmetic  5.78 us (8%)
  starting transfers between devices  5.75 us (8%)
  local copies, waits for them, and re-layouts  1.89 us (3%)
  between operations  1.52 us (2%)
    psum x1, blocking collectives, shards(): alpha = lax.psum(product(basis, applied), 'pos') / total_rows  14 us
    psum x1, blocking collectives, shards(): gram = lax.psum(product(residual, residual), 'pos') / total_rows  14 us
    all_gather x1, blocking collectives, shards(): lax.all_gather(partial_sum, 'grp')  11.7 us
    ppermute x4, waiting for transfers between devices, passed_along(): lax.ppermute(array, axis, [(i, (i + by) % peers) for i in range(peers)])  7.69 us
    ppermute x4, starting transfers between devices, passed_along(): lax.ppermute(array, axis, [(i, (i + by) % peers) for i in range(peers)])  5.75 us
    dot_general x1, matrix products, shards(): parts = jnp.einsum('kbj,kij->kbi', picked, blocks, precision=highest)  2.76 us
    another operation x2, other arithmetic, shards(): next_rows = jax.scipy.linalg.solve_triangular(factor, residual, lower=True)  2.47 us
    another operation x3, other arithmetic, shards(): factor = jnp.linalg.cholesky(gram)  2.13 us
  transfers between devices with their start and end apart: 4, of which 2 were waited for; matrix products, arithmetic and copies ran while one was open for 10% of the time, Pallas kernels for 0%

profile of v1, /device:TPU:0, one launch (start us, length us, event | category | flops | bytes accessed | tf_op | source)
XLA Modules:
  0.0 72.6 jit_solution(12245836137930768351)
XLA Ops:
  0.6 0.0 copy-start
  0.7 1.1 %copy.22 = f32[2,8,8,256]{3,2,1,0:T(8,128)S(1)} copy(f32[2,8,8,256]{3,1,2,0:T(8,128)} %bitcast.45) | data formatting | bytes 262144
  1.8 4.6 %collective-permute-start = (f32[16,8,256]{2,1,0:T(8,128)S(1)}, f32[16,8,256]{2,1,0:T(8,128)S(1)}, u32[]{:S(2)}, u32[]{:S(2)}) collective-permute-start(f32[16,8,256]{2,1,0:T(8,128)S(1)} %bitcast.46), channel_id=1, source_target_pairs={{0,7},{1,0},{2,1},{3,2},{4,3},{5,4},{6,5},{7,6},{8,15},{9,8},{10,9... | collective-permute-start | bytes 393224 | tf_op jit(solution)/shard_map/ppermute | solution.py:9
  7.0 1.1 %fusion.15 = f32[12,16,256]{2,0,1:T(8,128)S(1)} fusion(f32[16,8,256]{2,1,0:T(8,128)S(1)} %bitcast.47, s32[12]{0:T(128)} %bitcast.50, f32[12]{0:T(128)S(1)} %compare_convert_fusion), kind=kOutput, calls=%fused_computation.30 | convolution fusion | flops 4718784 | bytes 327776 | tf_op jit(solution)/shard_map/kt,bti->kbi/dot_general | solution.py:56
  8.1 1.7 %fusion = f32[12,16,256]{2,1,0:T(8,128)S(1)} fusion(f32[1,1,12,256,256]{4,3,2,1,0:T(8,128)S(1)} %copy-done, f32[12,16,256]{2,0,1:T(8,128)S(1)} %fusion.15), kind=kOutput, calls=%fused_computation | convolution fusion | flops 150994944 | bytes 3538944 | tf_op jit(solution)/shard_map/kbi,kij->kbj/dot_general | solution.py:57
  9.8 0.4 convolution_bitcast_fusion
  10.2 0.1 collective-permute-start.2
  10.4 1.1 %collective-permute-start.1 = (f32[16,8,256]{2,1,0:T(8,128)S(1)}, f32[16,8,256]{2,1,0:T(8,128)S(1)}, u32[]{:S(2)}, u32[]{:S(2)}) collective-permute-start(f32[16,8,256]{2,1,0:T(8,128)S(1)} %broadcast_select_fusion.1), channel_id=1, source_target_pairs={{0,6},{1,7},{2,0},{3,1},{4,2},{5,3},{6,4},{7,5},{8,14},{9,15},{10,... | collective-permute-start | bytes 393224 | tf_op jit(solution)/shard_map/ppermute | solution.py:9
  11.4 5.2 %collective-permute-done.2 = f32[16,8,256]{2,1,0:T(8,128)} collective-permute-done((f32[16,8,256]{2,1,0:T(8,128)S(1)}, f32[16,8,256]{2,1,0:T(8,128)}, u32[]{:S(2)}, u32[]{:S(2)}) %collective-permute-start.2) | collective-permute-done | bytes 131104 | tf_op jit(solution)/shard_map/ppermute | solution.py:9
  16.7 0.1 collective-permute-start.3
  16.8 0.0 collective-permute-done.1
  16.8 0.4 fusion.8
  17.2 0.0 copy-start.1
  17.2 0.0 copy-start.2
  17.2 2.8 %fusion.2 = f32[12,16,256]{2,1,0:T(8,128)S(1)} fusion(f32[1,1,12,256,256]{4,3,2,1,0:T(8,128)S(1)} %copy-done, f32[12,16,256]{2,0,1:T(8,128)S(1)} %fusion.8), kind=kOutput, calls=%fused_computation.2 | convolution fusion | flops 150994944 | bytes 3538944 | tf_op jit(solution)/shard_map/kbj,kij->kbi/dot_general | solution.py:54
  20.0 1.1 %convolution_bitcast_fusion.1 = f32[16,8,256]{2,1,0:T(8,128)S(1)} fusion(f32[12,16,256]{2,1,0:T(8,128)S(1)} %fusion.2, s32[12]{0:T(128)} %bitcast.51, f32[12]{0:T(128)S(1)} %compare_convert_fusion), kind=kOutput, calls=%fused_computation.7 | convolution fusion | flops 4718784 | bytes 327776 | tf_op jit(solution)/shard_map/kt,kbi->bti/dot_general | solution.py:55
  21.1 2.4 %collective-permute-done.3 = f32[16,8,256]{2,1,0:T(8,128)S(1)} collective-permute-done((f32[16,8,256]{2,1,0:T(8,128)S(1)}, f32[16,8,256]{2,1,0:T(8,128)S(1)}, u32[]{:S(2)}, u32[]{:S(2)}) %collective-permute-start.3) | collective-permute-done | bytes 131104 | tf_op jit(solution)/shard_map/ppermute | solution.py:9
  23.6 11.7 %all_gather.3 = f32[4,16,2048]{2,1,0:T(8,128)} all-gather(f32[1,16,2048]{2,1,0:T(8,128)S(1)} %all_gather_reshape.3), channel_id=1, replica_groups=mesh['grp'=4,'pos'=8] {'grp'}, dimensions={0}, use_global_device_ids=true | all-gather | bytes 655360 | tf_op jit(solution)/shard_map/all_gather | solution.py:62
  35.3 1.1 %reduce_sum.9 = f32[16,2048]{1,0:T(8,128)S(1)} reduce(f32[4,16,2048]{2,1,0:T(8,128)} %all_gather.3, f32[]{:T(128)} %constant.90.clone.1), dimensions={0}, to_apply=%region_0.1 | reduce | flops 98304 | bytes 655364 | tf_op jit(solution)/shard_map/reduce_sum | solution.py:62
  36.4 0.3 convolution_bitcast_fusion.2
  36.6 14.0 %psum.14 = f32[16,16]{0,1:T(8,128)S(1)} all-reduce(f32[16,16]{0,1:T(8,128)S(1)} %convolution_bitcast_fusion.2), channel_id=1, replica_groups=mesh['grp'=4,'pos'=8] {'pos'}, use_global_device_ids=true, to_apply=%region_1.2 | all-reduce | flops 256 | bytes 2048 | tf_op jit(solution)/shard_map/psum | solution.py:63
  50.6 0.3 convolution_subtract_fusion.1
  50.9 0.7 copy.16
  51.5 1.2 %convolution_subtract_fusion = f32[16,2048]{1,0:T(8,128)S(1)} fusion(f32[16,2048]{1,0:T(8,128)S(1)} %convolution_subtract_fusion.1, f32[16,16]{1,0:T(8,128)} %param.15, f32[16,2048]{1,0:T(8,128)} %param.14), kind=kOutput, calls=%fused_computation.4 | convolution fusion | flops 6324224 | bytes 394240 | tf_op jit(solution)/shard_map/dot_general | solution.py:13
  52.7 0.2 fusion.40
  53.0 14.0 %psum.15 = f32[16,16]{0,1:T(8,128)S(1)} all-reduce(f32[16,16]{0,1:T(8,128)S(1)} %fusion.40), channel_id=1, replica_groups=mesh['grp'=4,'pos'=8] {'pos'}, use_global_device_ids=true, to_apply=%region_2.3 | all-reduce | flops 256 | bytes 2048 | tf_op jit(solution)/shard_map/psum | solution.py:65
  66.9 0.1 copy.15
  67.0 1.5 %cholesky.16 = f32[16,16]{1,0:T(8,128)S(1)} custom-call(f32[16,16]{1,0:T(8,128)S(1)} %fusion.14), custom_call_target="Cholesky" | custom-call | tf_op jit(solution)/shard_map/jit(cholesky)/cholesky | solution.py:66
  68.5 0.6 compare_reduce_fusion
  69.2 1.2 %select_bitcast_fusion = (f32[1,16,16]{2,1,0:T(8,128)S(1)}, f32[16,16]{1,0:T(8,128)}) fusion(f32[16,16]{1,0:T(8,128)S(1)} %cholesky.16, pred[]{:T(512)} %compare_reduce_fusion), kind=kLoop, calls=%fused_computation.25 | loop fusion | flops 1024 | bytes 3073 | tf_op jit(solution)/shard_map/jit(_solve_triangular)/triangular_solve | solution.py:67
  70.4 1.2 %custom-call.7 = f32[1,16,16]{1,2,0:T(8,128)S(1)} custom-call(f32[1,16,16]{2,1,0:T(8,128)S(1)} %get-tuple-element.9), custom_call_target="InvertDiagBlocksLowerTriangular" | custom-call | tf_op jit(solution)/shard_map/jit(_solve_triangular)/triangular_solve | solution.py:67
  71.6 1.0 %fusion.12 = f32[16,2048]{1,0:T(8,128)} fusion(f32[16,2048]{1,0:T(8,128)S(1)} %convolution_subtract_fusion, f32[1,16,16]{1,2,0:T(8,128)S(1)} %custom-call.7), kind=kOutput, calls=%fused_computation.21 | convolution fusion | flops 6291456 | bytes 263168 | tf_op jit(solution)/shard_map/jit(_solve_triangular)/triangular_solve | solution.py:67
  (15 shorter events, 0.2 us)
Async XLA Ops:
  0.6 7.4 %copy-start = (f32[1,1,12,256,256]{4,3,2,1,0:T(8,128)S(1)}, f32[1,1,12,256,256]{4,3,2,1,0:T(8,128)}, u32[]{:S(2)}) copy-start(f32[1,1,12,256,256]{4,3,2,1,0:T(8,128)} %param.8) | copy-start | bytes 9437188
  0.6 9.1 %copy-start.3 = (s32[1,1,12]{2,1,0:T(1,128)S(1)}, s32[1,1,12]{2,1,0:T(1,128)}, u32[]{:S(2)}) copy-start(s32[1,1,12]{2,1,0:T(1,128)} %param.10) | copy-start | bytes 148
  1.8 8.6 %collective-permute-start = (f32[16,8,256]{2,1,0:T(8,128)S(1)}, f32[16,8,256]{2,1,0:T(8,128)S(1)}, u32[]{:S(2)}, u32[]{:S(2)}) collective-permute-start(f32[16,8,256]{2,1,0:T(8,128)S(1)} %bitcast.46), channel_id=1, source_target_pairs={{0,7},{1,0},{2,1},{3,2},{4,3},{5,4},{6,5},{7,6},{8,15},{9,8},{10,9... | collective-permute-start | bytes 393224 | tf_op jit(solution)/shard_map/ppermute | solution.py:9
  10.2 6.5 %collective-permute-start.2 = (f32[16,8,256]{2,1,0:T(8,128)S(1)}, f32[16,8,256]{2,1,0:T(8,128)}, u32[]{:S(2)}, u32[]{:S(2)}) collective-permute-start(f32[16,8,256]{2,1,0:T(8,128)S(1)} %convolution_bitcast_fusion), channel_id=1, source_target_pairs={{0,1},{1,2},{2,3},{3,4},{4,5},{5,6},{6,7},{7,0},{8,9},{9,10},{10,1... | collective-permute-start | bytes 393224 | tf_op jit(solution)/shard_map/ppermute | solution.py:9
  10.4 6.4 %collective-permute-start.1 = (f32[16,8,256]{2,1,0:T(8,128)S(1)}, f32[16,8,256]{2,1,0:T(8,128)S(1)}, u32[]{:S(2)}, u32[]{:S(2)}) collective-permute-start(f32[16,8,256]{2,1,0:T(8,128)S(1)} %broadcast_select_fusion.1), channel_id=1, source_target_pairs={{0,6},{1,7},{2,0},{3,1},{4,2},{5,3},{6,4},{7,5},{8,14},{9,15},{10,... | collective-permute-start | bytes 393224 | tf_op jit(solution)/shard_map/ppermute | solution.py:9
  16.7 6.8 %collective-permute-start.3 = (f32[16,8,256]{2,1,0:T(8,128)S(1)}, f32[16,8,256]{2,1,0:T(8,128)S(1)}, u32[]{:S(2)}, u32[]{:S(2)}) collective-permute-start(f32[16,8,256]{2,1,0:T(8,128)S(1)} %broadcast_select_fusion), channel_id=1, source_target_pairs={{0,2},{1,3},{2,4},{3,5},{4,6},{5,7},{6,0},{7,1},{8,10},{9,11},{10,... | collective-permute-start | bytes 393224 | tf_op jit(solution)/shard_map/ppermute | solution.py:9
  17.2 19.1 %copy-start.1 = (f32[16,2048]{1,0:T(8,128)S(1)}, f32[16,2048]{1,0:T(8,128)}, u32[]{:S(2)}) copy-start(f32[16,2048]{1,0:T(8,128)} %param.13) | copy-start | bytes 393220
  17.2 19.1 %copy-start.2 = (f32[2048]{0:T(1024)S(1)}, f32[2048]{0:T(1024)}, u32[]{:S(2)}) copy-start(f32[2048]{0:T(1024)} %param.12) | copy-start | bytes 24580
